TPU v7x, 32 devices: a whole 2x2x4 slice. The times are simulated.
32 devices in a mesh: ens: 4 (over x, core), state: 8 (over z, y).
Axes of the slice: x: 2, y: 2, z: 4, core: 2. Of those that a mesh axis runs over, the one named last changes fastest.
Arguments:
- ensemble: float32 [3072, 4096], P('state', 'ens'), may hold values from -18 to 18
- obs_values: float32 [2, 256], replicated, may hold values from -6 to 6
- obs_noise: bfloat16 [2, 256, 4096], P(None, None, 'ens'), may hold values from -6 to 6
- obs_var: float32 [2, 256], replicated, may hold values from 0.25 to 2
- obs_offset: int32 [2, 256], replicated, may hold values from 0 to 383, as said below
- owner: int32 [2], replicated, may hold values from 0 to 7
Outputs:
- analysis: float32 [3072, 4096], P('state', 'ens')
Inputs may be any that keep to these rules, and one draw needn't show every extreme that they name: `obs_offset`: the 256 offsets of one batch are distinct.
All inputs are finite; a program needn't handle non-finite values.
Results may differ from a plain program's by a relative error of at most 0.0003.
Values sent between devices are 32-bit elements; how exact they have to be, the bound alone decides.
A program may use at most 64 MiB of HBM per device.

v0:
```python
import jax
import jax.numpy as jnp
from jax import lax
from jax.sharding import PartitionSpec as P

NB = 2


finest = lax.Precision.HIGHEST


def cycle_taper(first, second, total, reach):
    distance = jnp.abs(first - second)
    distance = jnp.minimum(distance, total - distance).astype(jnp.float32)
    ratio = distance / jnp.float32(reach)
    return 1.0 / (1.0 + ratio * ratio)


def obs_moments(obs_prior, members):
    row_total = lax.psum(jnp.sum(obs_prior, axis=1), "ens")
    obs_anom = obs_prior - (row_total / members)[:, None]
    spread = lax.psum(jnp.einsum("pm,qm->pq", obs_anom, obs_anom, precision=finest), "ens")
    return (obs_anom, spread)


def innovations(obs_prior, spread, places, states, reach, members, values, variance, noise):
    obs_cov = cycle_taper(places[:, None], places[None, :], states, reach) * (
        spread / (members - 1)
    ) + jnp.diag(variance)
    factor = jnp.linalg.cholesky(obs_cov)
    misfit = values[:, None] + jnp.sqrt(variance)[:, None] * noise.astype(jnp.float32) - obs_prior
    return jax.scipy.linalg.cho_solve((factor, True), misfit)


def local(ensemble, obs_values, obs_noise, obs_var, obs_offset, owner):
    rows, width = ensemble.shape
    members = width * lax.axis_size("ens")
    states = rows * lax.axis_size("state")
    reach = states // 4
    here = lax.axis_index("state")
    positions = here * rows + jnp.arange(rows, dtype=jnp.int32)
    current = ensemble
    for batch in range(NB):
        places = owner[batch] * rows + obs_offset[batch]
        local_rows = jnp.take(current, obs_offset[batch], axis=0)
        is_owner = here == owner[batch]
        masked_rows = jnp.where(is_owner, local_rows, 0.0)
        obs_prior = lax.psum(masked_rows, "state")
        obs_anom, spread = obs_moments(obs_prior, members)
        solved = innovations(
            obs_prior,
            spread,
            places,
            states,
            reach,
            members,
            obs_values[batch],
            obs_var[batch],
            obs_noise[batch],
        )
        partial_cov = jnp.einsum("sm,pm->sp", current, obs_anom, precision=finest)
        cross = lax.psum(partial_cov, "ens")
        gain = cycle_taper(positions[:, None], places[None, :], states, reach) * (
            cross / (members - 1)
        )
        current = current + jnp.dot(
            gain, solved, precision=finest, preferred_element_type=jnp.float32
        )
    return current


def solution(mesh):
    in_specs = (P("state", "ens"), P(), P(None, None, "ens"), P(), P(), P())
    out_specs = P("state", "ens")
    return jax.shard_map(local, mesh=mesh, in_specs=in_specs, out_specs=out_specs, check_vma=False)
```

profile of v0, /device:TPU:0, one launch (start us, length us, event | category | flops | bytes accessed | tf_op | source)
XLA Modules:
  0.0 414.6 jit_solution(4110207383472466906)
XLA Ops:
  6.5 1.4 fusion.105
  9.3 0.8 broadcast_add_fusion.1
  10.7 3.0 gather_fusion
  13.7 1.1 select_select_fusion.1
  15.8 80.3 %all-reduce.8.cloned.1.call-done = f32[256,1024]{1,0:T(8,128)} async-done(((f32[256,1024]{1,0:T(8,128)}), f32[256,1024]{1,0:T(8,128)}) %all-reduce.8.cloned.1.call-update) | async-done | bytes 1048592 | tf_op jit(solution)/shard_map/psum | solution.py:48
  96.2 1.8 fusion.102
  97.9 6.5 %psum.57 = f32[256]{0:T(256)S(1)} all-reduce(f32[256]{0:T(256)S(1)} %get-tuple-element.50), channel_id=1, replica_groups=mesh['ens'=4,'state'=8] {'ens'}, use_global_device_ids=true, to_apply=%region_2.4 | all-reduce | flops 256 | bytes 2048 | tf_op jit(solution)/shard_map/psum | solution.py:20
  104.4 3.6 convolution_bitcast_fusion
  108.0 1.9 fusion.14
  110.5 32.7 %all-reduce.14.cloned.1.call-done = (f32[256,256]{0,1:T(8,128)}, f32[384,256]{1,0:T(8,128)}) async-done(((f32[256,256]{0,1:T(8,128)}, f32[384,256]{1,0:T(8,128)}), (f32[256,256]{0,1:T(8,128)}, f32[384,256]{1,0:T(8,128)})) %all-reduce.14.cloned.1.call-update) | async-done | bytes 655376 | tf_op jit(solution)/shard_map/psum | solution.py:22
  143.2 1.1 fusion.51
  144.5 1.2 fusion.60
  145.6 11.7 %cholesky.130 = f32[128,128]{1,0:T(8,128)S(1)} custom-call(f32[128,128]{1,0:T(8,128)S(1)} %cholesky.194), custom_call_target="Cholesky" | custom-call | tf_op jit(solution)/shard_map/jit(cholesky)/cholesky | solution.py:30
  157.4 9.8 %custom-call.15 = f32[1,128,128]{1,2,0:T(8,128)S(1)} custom-call(f32[1,128,128]{2,1,0:T(8,128)S(1)} %get-tuple-element.59), custom_call_target="InvertDiagBlocksLowerTriangular" | custom-call | tf_op jit(solution)/shard_map/jit(cholesky)/cholesky | solution.py:30
  167.7 11.7 %cholesky.147 = f32[128,128]{1,0:T(8,128)S(1)} custom-call(f32[128,128]{1,0:T(8,128)S(1)} %convolution_subtract_fusion.5), custom_call_target="Cholesky" | custom-call | tf_op jit(solution)/shard_map/jit(cholesky)/cholesky | solution.py:30
  179.5 0.7 compare_reduce_fusion.2
  181.6 4.1 while.4
  181.8 0.6 fusion.124
  182.4 1.4 bitcast_dynamic-update-slice_fusion.4
  184.3 1.4 bitcast_dynamic-update-slice_fusion.4
  185.7 19.7 %custom-call.16 = f32[2,128,128]{1,2,0:T(8,128)S(1)} custom-call(f32[2,128,128]{2,1,0:T(8,128)S(1)} %get-tuple-element.22), custom_call_target="InvertDiagBlocksLowerTriangular" | custom-call | tf_op jit(solution)/shard_map/jit(_cho_solve)/triangular_solve | solution.py:32
  205.4 0.6 fusion.19
  206.6 0.6 fusion.81
  207.9 0.6 convolution_subtract_fusion.2
  209.1 1.6 convolution_add_fusion.1
  210.7 1.1 gather_fusion.1
  211.8 1.1 select_select_fusion
  213.0 78.4 %all-reduce.10.cloned.1.call-done = f32[256,1024]{1,0:T(8,128)} async-done(((f32[256,1024]{1,0:T(8,128)}), f32[256,1024]{1,0:T(8,128)}) %all-reduce.10.cloned.1.call-update) | async-done | bytes 1048592 | tf_op jit(solution)/shard_map/psum | solution.py:48
  291.4 1.8 fusion.101
  293.1 6.7 %psum.61 = f32[256]{0:T(256)S(1)} all-reduce(f32[256]{0:T(256)S(1)} %get-tuple-element.48), channel_id=1, replica_groups=mesh['ens'=4,'state'=8] {'ens'}, use_global_device_ids=true, to_apply=%region_11.15 | all-reduce | flops 256 | bytes 2048 | tf_op jit(solution)/shard_map/psum | solution.py:20
  299.9 3.6 fusion.12
  303.4 1.9 fusion.10
  305.3 33.2 %all-reduce.12.cloned.1.call-done = (f32[256,256]{0,1:T(8,128)}, f32[384,256]{1,0:T(8,128)}) async-done(((f32[256,256]{0,1:T(8,128)}, f32[384,256]{1,0:T(8,128)}), (f32[256,256]{0,1:T(8,128)}, f32[384,256]{1,0:T(8,128)})) %all-reduce.12.cloned.1.call-update) | async-done | bytes 655376 | tf_op jit(solution)/shard_map/psum | solution.py:22
  338.5 1.1 fusion.58
  339.8 1.2 fusion.59
  341.0 11.7 %cholesky.164 = f32[128,128]{1,0:T(8,128)S(1)} custom-call(f32[128,128]{1,0:T(8,128)S(1)} %cholesky.197), custom_call_target="Cholesky" | custom-call | tf_op jit(solution)/shard_map/jit(cholesky)/cholesky | solution.py:30
  352.8 9.8 %custom-call.17 = f32[1,128,128]{1,2,0:T(8,128)S(1)} custom-call(f32[1,128,128]{2,1,0:T(8,128)S(1)} %get-tuple-element.55), custom_call_target="InvertDiagBlocksLowerTriangular" | custom-call | tf_op jit(solution)/shard_map/jit(cholesky)/cholesky | solution.py:30
  363.1 11.9 %cholesky.181 = f32[128,128]{1,0:T(8,128)S(1)} custom-call(f32[128,128]{1,0:T(8,128)S(1)} %convolution_subtract_fusion.4), custom_call_target="Cholesky" | custom-call | tf_op jit(solution)/shard_map/jit(cholesky)/cholesky | solution.py:30
  375.1 0.7 compare_reduce_fusion
  375.8 0.6 compare_reduce_fusion.1
  377.7 4.0 while.5
  378.3 1.4 bitcast_dynamic-update-slice_fusion.5
  380.3 1.4 bitcast_dynamic-update-slice_fusion.5
  381.7 19.7 %custom-call.18 = f32[2,128,128]{1,2,0:T(8,128)S(1)} custom-call(f32[2,128,128]{2,1,0:T(8,128)S(1)} %get-tuple-element.23), custom_call_target="InvertDiagBlocksLowerTriangular" | custom-call | tf_op jit(solution)/shard_map/jit(_cho_solve)/triangular_solve | solution.py:32
  401.4 0.6 fusion.17
  402.6 0.6 fusion.84
  403.9 0.6 convolution_subtract_fusion
  405.1 2.7 convolution_add_fusion
  (68 shorter events, 7.6 us)
Async XLA Ops:
  6.5 89.6 %all-reduce.8.cloned.1.call-start = ((), (), s32[]{:S(2)}) async-start(), calls=%async_computation | async-start | bytes 2097152 | tf_op jit(solution)/shard_map/psum | solution.py:48
  13.7 2.0 copy-start.5
  13.7 2.1 copy-start.6
  14.9 89.6 %copy-start = (f32[384,1024]{1,0:T(8,128)S(1)}, f32[384,1024]{1,0:T(8,128)}, u32[]{:S(2)}) copy-start(f32[384,1024]{1,0:T(8,128)} %param.11) | copy-start | bytes 4718596
  14.9 128.3 %all-reduce.14.cloned.1.call-start = ((), (), s32[]{:S(2)}) async-start(), calls=%async_computation.3 | async-start | bytes 1310720 | tf_op jit(solution)/shard_map/psum | solution.py:22
  104.4 3.6 copy-start.1
  109.9 181.5 %all-reduce.10.cloned.1.call-start = ((), (), s32[]{:S(2)}) async-start(), calls=%async_computation.1 | async-start | bytes 2097152 | tf_op jit(solution)/shard_map/psum | solution.py:48
  207.8 1.3 copy-start.3
  212.9 125.6 %all-reduce.12.cloned.1.call-start = ((), (), s32[]{:S(2)}) async-start(), calls=%async_computation.2 | async-start | bytes 1310720 | tf_op jit(solution)/shard_map/psum | solution.py:22
  299.8 3.6 copy-start.2
  403.8 1.2 copy-start.4
Sparse Core Ops, SparseCore 0:
  15.0 81.0 all-reduce.7
  110.0 33.0 all-reduce.13
  213.1 78.2 all-reduce.9
  305.4 33.0 all-reduce.11
where the time goes:
time: 419 us; the launch traced here: 415 us
  waiting for transfers between devices  225 us (54%)
  other arithmetic  120 us (29%)
  matrix products  23.4 us (6%)
  between operations  19.2 us (5%)
  local copies, waits for them, and re-layouts  13.7 us (3%)
  blocking collectives  13.2 us (3%)
    psum x2, waiting for transfers between devices, local(): obs_prior = lax.psum(masked_rows, 'state')  159 us
    another operation x13, other arithmetic, innovations(): factor = jnp.linalg.cholesky(obs_cov)  68.9 us
    psum x2, waiting for transfers between devices, obs_moments(): lax.psum(jnp.einsum('pm,qm->pq', obs_anom, obs_anom, precision=finest), '...  65.9 us
    another operation x5, other arithmetic, innovations(): return jax.scipy.linalg.cho_solve((factor, True), misfit)  39.4 us
    psum x2, blocking collectives, obs_moments(): row_total = lax.psum(jnp.sum(obs_prior, axis=1), 'ens')  13.2 us
  transfers between devices with their start and end apart: 4, of which 4 were waited for; matrix products, arithmetic and copies ran while one was open for 0% of the time, Pallas kernels for 0%

commit v1 on v0

v1 whole, which is shorter than its diff:
```python
import functools

import jax
import jax.numpy as jnp
from jax import lax
from jax.experimental import pallas as pl
from jax.experimental.pallas import tpu as pltpu
from jax.sharding import PartitionSpec as P

NB = 2
LAG = 3
CHUNKS = 16
SUM_CHUNKS = 4
MESH = pl.DeviceIdType.MESH
finest = lax.Precision.HIGHEST


def cycle_taper(first, second, total, reach):
    distance = jnp.abs(first - second)
    distance = jnp.minimum(distance, total - distance).astype(jnp.float32)
    ratio = distance / jnp.float32(reach)
    return 1.0 / (1.0 + ratio * ratio)


def spread_kernel(
    n_state, n_ens,
    own, sums, out, sums_out,
    right_in, left_in, right_out, left_out, total, side_in, ens_in, ens_total, state_in,
    right_send, right_recv, left_send, left_recv, side_send, side_recv,
    ens_send, ens_recv, state_send, state_recv,
):
    rows = own.shape[0] // CHUNKS
    here = lax.axis_index("state")
    ens = lax.axis_index("ens")
    last = n_state // 2 - 1
    place = here // 2
    side = here + 1 - 2 * lax.rem(here, 2)

    barrier = pltpu.get_barrier_semaphore()
    for step in range(1, n_ens):
        pl.semaphore_signal(
            barrier, inc=1, device_id={"ens": lax.rem(ens + step, n_ens)}, device_id_type=MESH
        )
    for step in range(1, n_state):
        pl.semaphore_signal(
            barrier, inc=1, device_id={"state": lax.rem(here + step, n_state)}, device_id_type=MESH
        )
    pl.semaphore_wait(barrier, n_ens + n_state - 2)

    def remote(src, dst, send, recv, target):
        return pltpu.make_async_remote_copy(
            src_ref=src, dst_ref=dst, send_sem=send, recv_sem=recv,
            device_id=target, device_id_type=MESH,
        )

    def ens_copy(step):
        return remote(
            sums, ens_in.at[step - 1], ens_send.at[step - 1], ens_recv.at[step - 1],
            {"ens": lax.rem(ens + step, n_ens)},
        )

    def state_copy(step):
        return remote(
            ens_total, state_in.at[step - 1], state_send.at[step - 1], state_recv.at[step - 1],
            {"state": lax.rem(here + step, n_state)},
        )

    def span(c):
        return pl.ds(pl.multiple_of(c * rows, rows), rows)

    def right_copy(src, c):
        return remote(
            src.at[span(c)], right_in.at[span(c)], right_send.at[c], right_recv.at[c],
            {"state": lax.rem(here + 2, n_state)},
        )

    def left_copy(src, c):
        return remote(
            src.at[span(c)], left_in.at[span(c)], left_send.at[c], left_recv.at[c],
            {"state": lax.rem(here + n_state - 2, n_state)},
        )

    def side_copy(c):
        return remote(
            total.at[span(c)], side_in.at[span(c)], side_send.at[c], side_recv.at[c],
            {"state": side},
        )

    def each(body):
        lax.fori_loop(0, CHUNKS, lambda c, carry: (body(c), carry)[1], 0)

    for step in range(1, n_ens):
        ens_copy(step).start()
    if last > 0:
        @pl.when(place == 0)
        def _():
            each(lambda c: right_copy(own, c).start())

        @pl.when(place == last)
        def _():
            each(lambda c: left_copy(own, c).start())

    for step in range(1, n_ens):
        ens_copy(step).wait_recv()
    whole = sums[...]
    for step in range(1, n_ens):
        whole = whole + ens_in[step - 1]
    ens_total[...] = whole
    for step in range(1, n_state):
        state_copy(step).start()

    def right_step(c):
        @pl.when(place > 0)
        def _():
            right_copy(own, c).wait_recv()
            right_out[span(c)] = own[span(c)] + right_in[span(c)]

            @pl.when(place < last)
            def _():
                right_copy(right_out, c).start()

    def left_step(c):
        @pl.when(place < last)
        def _():
            left_copy(own, c).wait_recv()
            left_out[span(c)] = own[span(c)] + left_in[span(c)]

            @pl.when(place > 0)
            def _():
                left_copy(left_out, c).start()

    def turn(t, carry):
        late = t - LAG

        @pl.when(t < CHUNKS)
        def _():
            @pl.when(2 * place <= last)
            def _():
                right_step(t)

            @pl.when(2 * place > last)
            def _():
                left_step(t)

        @pl.when(late >= 0)
        def _():
            @pl.when(2 * place <= last)
            def _():
                left_step(late)

            @pl.when(2 * place > last)
            def _():
                right_step(late)

            if last == 0:
                total[span(late)] = own[span(late)]
            else:
                @pl.when(place == 0)
                def _():
                    total[span(late)] = left_out[span(late)]

                @pl.when(place == last)
                def _():
                    total[span(late)] = right_out[span(late)]

                @pl.when((place > 0) & (place < last))
                def _():
                    total[span(late)] = right_out[span(late)] + left_in[span(late)]

            side_copy(late).start()

        return carry

    lax.fori_loop(0, CHUNKS + LAG, turn, 0)

    def finish(c):
        side_copy(c).wait_recv()
        out[span(c)] = total[span(c)] + side_in[span(c)]

    each(finish)
    for step in range(1, n_state):
        state_copy(step).wait_recv()
    whole = ens_total[...]
    for step in range(1, n_state):
        whole = whole + state_in[step - 1]
    sums_out[...] = whole

    for step in range(1, n_ens):
        ens_copy(step).wait_send()
    for step in range(1, n_state):
        state_copy(step).wait_send()
    each(lambda c: side_copy(c).wait_send())

    @pl.when(place < last)
    def _():
        each(lambda c: right_copy(own, c).wait_send())

    @pl.when(place > 0)
    def _():
        each(lambda c: left_copy(own, c).wait_send())


def spread_call(n_state, n_ens, own, sums):
    vmem = pl.BlockSpec(memory_space=pltpu.VMEM)
    big = pltpu.VMEM(own.shape, own.dtype)
    dma = pltpu.SemaphoreType.DMA
    return pl.pallas_call(
        functools.partial(spread_kernel, n_state, n_ens),
        out_shape=(
            jax.ShapeDtypeStruct(own.shape, own.dtype),
            jax.ShapeDtypeStruct(sums.shape, sums.dtype),
        ),
        in_specs=[vmem] * 2,
        out_specs=(vmem, vmem),
        scratch_shapes=[big] * 6
        + [
            pltpu.VMEM((n_ens - 1,) + sums.shape, sums.dtype),
            pltpu.VMEM(sums.shape, sums.dtype),
            pltpu.VMEM((n_state - 1,) + sums.shape, sums.dtype),
        ]
        + [dma((CHUNKS,))] * 6
        + [dma((n_ens - 1,))] * 2
        + [dma((n_state - 1,))] * 2,
        compiler_params=pltpu.CompilerParams(
            collective_id=0, has_side_effects=True, vmem_limit_bytes=40 * 2**20
        ),
        name="spread",
    )(own, sums)


def sum_kernel(n_ens, part, out, pair_in, step_out, step_in, back_out, back_in, *sems):
    half = part.shape[0] // 2
    rows = half // SUM_CHUNKS
    ens = lax.axis_index("ens")
    low = lax.rem(ens, 2)
    bits = [1]
    while bits[-1] * 2 < n_ens:
        bits.append(bits[-1] * 2)

    def partner(bit):
        return {"ens": ens + bit - 2 * bit * lax.rem(ens // bit, 2)}

    barrier = pltpu.get_barrier_semaphore()
    for bit in bits:
        pl.semaphore_signal(barrier, inc=1, device_id=partner(bit), device_id_type=MESH)
    pl.semaphore_wait(barrier, len(bits))

    def remote(src, dst, which, c, bit):
        return pltpu.make_async_remote_copy(
            src_ref=src, dst_ref=dst,
            send_sem=sems[which].at[0, c], recv_sem=sems[which].at[1, c],
            device_id=partner(bit), device_id_type=MESH,
        )

    def span(c, base=0):
        return pl.ds(pl.multiple_of(base * half + c * rows, rows), rows)

    def pair_copy(c):
        return remote(part.at[span(c, 1 - low)], pair_in.at[span(c)], 0, c, 1)

    def step_copy(i, c):
        return remote(step_out.at[i, span(c)], step_in.at[i, span(c)], 2 + i, c, bits[i + 1])

    def back_copy(c):
        return remote(back_out.at[span(c)], back_in.at[span(c)], 1, c, 1)

    steps = len(bits) - 1
    for c in range(SUM_CHUNKS):
        pair_copy(c).start()
    for c in range(SUM_CHUNKS):
        pair_copy(c).wait_recv()
        value = part[span(c, low)] + pair_in[span(c)]
        if steps:
            step_out[0, span(c)] = value
            step_copy(0, c).start()
        else:
            back_out[span(c)] = value
            back_copy(c).start()
    for i in range(steps):
        for c in range(SUM_CHUNKS):
            step_copy(i, c).wait_recv()
            value = step_out[i, span(c)] + step_in[i, span(c)]
            if i + 1 < steps:
                step_out[i + 1, span(c)] = value
                step_copy(i + 1, c).start()
            else:
                back_out[span(c)] = value
                back_copy(c).start()
    for c in range(SUM_CHUNKS):
        out[span(c, low)] = back_out[span(c)]
    for c in range(SUM_CHUNKS):
        back_copy(c).wait_recv()
        out[span(c, 1 - low)] = back_in[span(c)]
    for c in range(SUM_CHUNKS):
        pair_copy(c).wait_send()
        back_copy(c).wait_send()
        for i in range(steps):
            step_copy(i, c).wait_send()


def sum_call(n_ens, part):
    vmem = pl.BlockSpec(memory_space=pltpu.VMEM)
    half = (part.shape[0] // 2, part.shape[1])
    steps = max(1, (n_ens - 1).bit_length() - 1)
    dma = pltpu.SemaphoreType.DMA
    return pl.pallas_call(
        functools.partial(sum_kernel, n_ens),
        out_shape=jax.ShapeDtypeStruct(part.shape, part.dtype),
        in_specs=[vmem],
        out_specs=vmem,
        scratch_shapes=[
            pltpu.VMEM(half, part.dtype),
            pltpu.VMEM((steps,) + half, part.dtype),
            pltpu.VMEM((steps,) + half, part.dtype),
            pltpu.VMEM(half, part.dtype),
            pltpu.VMEM(half, part.dtype),
        ]
        + [dma((2, SUM_CHUNKS))] * (2 + steps),
        compiler_params=pltpu.CompilerParams(
            collective_id=1, has_side_effects=True, vmem_limit_bytes=32 * 2**20
        ),
        name="ens_sum",
    )(part)


def mul(a, b):
    return jnp.dot(a, b, precision=finest, preferred_element_type=jnp.float32)


def invert(a):
    size = a.shape[0]
    across = lax.broadcasted_iota(jnp.int32, (1, size), 1)
    down = lax.broadcasted_iota(jnp.int32, (size, 1), 0)
    for k in range(size):
        column = a[:, k : k + 1]
        pivot = 1.0 / a[k : k + 1, k : k + 1]
        row = jnp.where(across == k, 1.0, a[k : k + 1, :]) * pivot
        rest = jnp.where(across == k, 0.0, a) - column * row
        a = jnp.where(down == k, row, rest)
    return a


def solve_kernel(moments, scale, diagonal, out):
    size = moments.shape[0]
    half = size // 2
    cov = moments[:, :size] * scale[:, :size] + diagonal[...]
    right = moments[:, size:] * scale[:, size:]
    corner = invert(cov[:half, :half])
    cross = cov[:half, half:]
    across = mul(corner, cross)
    rest = invert(cov[half:, half:] - mul(cross.T, across))
    first = mul(corner, right[:half])
    second = mul(rest, right[half:] - mul(cross.T, first))
    out[half:] = second
    out[:half] = first - mul(across, second)


def solve_call(moments, scale, diagonal):
    vmem = pl.BlockSpec(memory_space=pltpu.VMEM)
    size = moments.shape[0]
    return pl.pallas_call(
        solve_kernel,
        out_shape=jax.ShapeDtypeStruct((size, moments.shape[1] - size), jnp.float32),
        in_specs=[vmem] * 3,
        out_specs=vmem,
        compiler_params=pltpu.CompilerParams(vmem_limit_bytes=32 * 2**20),
        name="gain",
    )(moments, scale, diagonal)


def local(ensemble, obs_values, obs_noise, obs_var, obs_offset, owner):
    rows, width = ensemble.shape
    n_ens = lax.axis_size("ens")
    n_state = lax.axis_size("state")
    members = width * n_ens
    states = rows * n_state
    reach = states // 4
    here = lax.axis_index("state")
    positions = here * rows + jnp.arange(rows, dtype=jnp.int32)
    current = ensemble
    for batch in range(NB):
        places = owner[batch] * rows + obs_offset[batch]
        aims = jnp.concatenate([places, positions])
        scale = cycle_taper(places[:, None], aims[None, :], states, reach) / (members - 1)
        diagonal = jnp.diag(obs_var[batch])
        local_rows = jnp.take(current, obs_offset[batch], axis=0)
        masked = jnp.where(here == owner[batch], local_rows, 0.0)
        sums = jnp.broadcast_to(jnp.sum(masked, axis=1)[None, :], (8, masked.shape[0]))
        prior, totals = spread_call(n_state, n_ens, masked, sums)
        anom = prior - (totals[0] / members)[:, None]
        spread = jnp.einsum("pm,qm->pq", anom, anom, precision=finest)
        cross = jnp.einsum("pm,sm->ps", anom, current, precision=finest)
        moments = sum_call(n_ens, jnp.concatenate([spread, cross], axis=1))
        gain = solve_call(moments, scale, diagonal)
        variance = obs_var[batch]
        misfit = (
            obs_values[batch][:, None]
            + jnp.sqrt(variance)[:, None] * obs_noise[batch].astype(jnp.float32)
            - prior
        )
        current = current + jnp.einsum("ps,pm->sm", gain, misfit, precision=finest)
    return current


def solution(mesh):
    in_specs = (P("state", "ens"), P(), P(None, None, "ens"), P(), P(), P())
    out_specs = P("state", "ens")
    return jax.shard_map(local, mesh=mesh, in_specs=in_specs, out_specs=out_specs, check_vma=False)
```

time: 419 us -> 174 us (0.42); the launches traced: 415 us -> 174 us
  waiting for transfers between devices: 225 us -> 0 us
  Pallas kernels: 0 us -> 153 us
  other arithmetic: 120 us -> 1.47 us
  between operations: 19.2 us -> 2.92 us
  blocking collectives: 13.2 us -> 0 us
  matrix products: 23.4 us -> 10.7 us
  local copies, waits for them, and re-layouts: 13.7 us -> 6.19 us
    psum x4 -> x0, waiting for transfers between devices: 225 us -> none  [the longest x2 159 us: local(): obs_prior = lax.psum(masked_rows, 'state')]
    pallas_call x0 -> x6, Pallas kernels: none -> 153 us  [the longest x2 81.7 us: spread_call(): pl.pallas_call(functools.partial(spread_kernel, n_state, n_ens), out_shap...]
    another operation x18 -> x0, other arithmetic: 108 us -> none  [the longest x13 68.9 us: innovations(): factor = jnp.linalg.cholesky(obs_cov)]
    psum x2 -> x0, blocking collectives: 13.2 us -> none  [obs_moments(): row_total = lax.psum(jnp.sum(obs_prior, axis=1), 'ens')]
    another operation x16 -> x0, matrix products: 8.23 us -> none  [the longest x12 7.29 us: innovations(): return jax.scipy.linalg.cho_solve((factor, True), misfit)]
    another operation x19 -> x0, local copies, waits for them, and re-layouts: 7.95 us -> none  [the longest x15 7.9 us: innovations(): return jax.scipy.linalg.cho_solve((factor, True), misfit)]
    dot_general x6, matrix products: 15.2 us -> 10.7 us  [the longest x2 4.5 us: local(): current = current + jnp.einsum('ps,pm->sm', gain, misfit, precision=finest)]
  transfers between devices with their start and end apart: 4 -> 0, of which waited for: 4 -> 0; matrix products, arithmetic and copies ran while one was open for 0% -> 0% of each run, Pallas kernels for 0% -> 0%
where the time goes in v1:
time: 174 us
  Pallas kernels  153 us (88%)
  matrix products  10.7 us (6%)
  local copies, waits for them, and re-layouts  6.19 us (4%)
  between operations  2.92 us (2%)
    pallas_call x2, Pallas kernels, spread_call(): pl.pallas_call(functools.partial(spread_kernel, n_state, n_ens), out_shap...  81.7 us
    pallas_call x2, Pallas kernels, solve_call(): pl.pallas_call(solve_kernel, out_shape=jax.ShapeDtypeStruct((size, moment...  46.2 us
    pallas_call x2, Pallas kernels, sum_call(): pl.pallas_call(functools.partial(sum_kernel, n_ens), out_shape=jax.ShapeD...  24.7 us
    dot_general x2, matrix products, local(): current = current + jnp.einsum('ps,pm->sm', gain, misfit, precision=finest)  4.5 us
    gather x2, local copies, waits for them, and re-layouts, local(): local_rows = jnp.take(current, obs_offset[batch], axis=0)  4.05 us
    dot_general x2, matrix products, local(): cross = jnp.einsum('pm,sm->ps', anom, current, precision=finest)  3.92 us

profile of v1, /device:TPU:0, one launch (start us, length us, event | category | flops | bytes accessed | tf_op | source)
XLA Modules:
  0.0 173.9 jit_solution(14545103786535348331)
XLA Ops:
  0.0 0.8 fusion.44
  0.8 1.3 fusion.45
  2.7 3.0 %gather_fusion = f32[256,1024]{1,0:T(8,128)S(1)} fusion(f32[384,1024]{1,0:T(8,128)} %param.8, s32[1024]{0:T(1024)S(1)} %pad_clamp_fusion.1), kind=kCustom, calls=%fused_computation.clone | custom fusion | bytes 2098176 | tf_op jit(solution)/shard_map/jit(_take)/gather | solution.py:386
  6.4 0.3 fusion.41
  6.6 0.0 copy-start
  6.7 42.6 %spread.2 = (f32[256,1024]{1,0:T(8,128)S(1)}, f32[8,256]{1,0:T(8,128)S(1)}) custom-call(f32[256,1024]{1,0:T(8,128)S(1)} %get-tuple-element.17.own, f32[8,256]{1,0:T(8,128)S(1)} %broadcast_in_dim.64.sums), custom_call_target="tpu_custom_call" | custom-call | tf_op jit(solution)/shard_map/spread/pallas_call | solution.py:207
  49.3 1.1 fusion.12
  50.4 0.0 copy-done
  50.4 1.9 %fusion.10 = f32[256,384]{1,0:T(8,128)S(1)} fusion(f32[384,1024]{1,0:T(8,128)S(1)} %copy-done, f32[256,1024]{1,0:T(8,128)S(1)} %get-tuple-element.10, f32[256]{0:T(256)S(1)} %bitcast.33), kind=kOutput, calls=%fused_computation.16 | convolution fusion | flops 1208221696 | bytes 3015680 | tf_op jit(solution)/shard_map/pm,sm->ps/dot_general | solution.py:392
  52.4 0.0 copy-start.4
  52.4 12.4 %ens_sum.2.moments = f32[256,640]{1,0:T(8,128)S(1)} custom-call(f32[256,640]{1,0:T(8,128)S(1)} %pad_maximum_fusion.part), custom_call_target="tpu_custom_call" | custom-call | tf_op jit(solution)/shard_map/ens_sum/pallas_call | solution.py:306
  65.5 0.0 copy-start.5
  65.5 0.0 copy-start.1
  65.5 0.0 copy-start.2
  65.6 0.6 fusion.19
  66.2 0.0 copy-done.4
  66.2 0.1 fusion.39.diagonal
  66.3 23.1 %gain.2 = f32[256,384]{1,0:T(8,128)S(1)} custom-call(f32[256,640]{1,0:T(8,128)S(1)} %ens_sum.2.moments, f32[256,640]{1,0:T(8,128)S(1)} %get-tuple-element.32.scale, f32[256,256]{1,0:T(8,128)S(1)} %fusion.39.diagonal), custom_call_target="tpu_custom_call" | custom-call | tf_op jit(solution)/shard_map/gain/pallas_call | solution.py:361
  89.4 0.0 copy-done.5
  89.4 0.0 copy-done.1
  89.4 0.0 copy-done.2
  89.4 1.7 convolution_add_fusion.1
  91.1 1.1 gather_fusion.1
  92.9 0.3 fusion.40
  93.1 39.2 %spread.3 = (f32[256,1024]{1,0:T(8,128)S(1)}, f32[8,256]{1,0:T(8,128)S(1)}) custom-call(f32[256,1024]{1,0:T(8,128)S(1)} %get-tuple-element.15.own, f32[8,256]{1,0:T(8,128)S(1)} %broadcast_in_dim.68.sums), custom_call_target="tpu_custom_call" | custom-call | tf_op jit(solution)/shard_map/spread/pallas_call | solution.py:207
  132.3 1.2 fusion.8
  133.5 2.0 %fusion.6 = f32[256,384]{1,0:T(8,128)S(1)} fusion(f32[384,1024]{1,0:T(8,128)S(1)} %convolution_add_fusion.1, f32[256,1024]{1,0:T(8,128)S(1)} %get-tuple-element.12, f32[256]{0:T(256)S(1)} %bitcast.31), kind=kOutput, calls=%fused_computation.12 | convolution fusion | flops 1208221696 | bytes 3015680 | tf_op jit(solution)/shard_map/pm,sm->ps/dot_general | solution.py:392
  135.5 0.0 copy-start.3
  135.5 12.3 %ens_sum.3.moments = f32[256,640]{1,0:T(8,128)S(1)} custom-call(f32[256,640]{1,0:T(8,128)S(1)} %pad_maximum_fusion.1.part), custom_call_target="tpu_custom_call" | custom-call | tf_op jit(solution)/shard_map/ens_sum/pallas_call | solution.py:306
  147.9 0.1 fusion.38.diagonal
  148.0 23.1 %gain.3 = f32[256,384]{1,0:T(8,128)S(1)} custom-call(f32[256,640]{1,0:T(8,128)S(1)} %ens_sum.3.moments, f32[256,640]{1,0:T(8,128)S(1)} %get-tuple-element.33.scale, f32[256,256]{1,0:T(8,128)S(1)} %fusion.38.diagonal), custom_call_target="tpu_custom_call" | custom-call | tf_op jit(solution)/shard_map/gain/pallas_call | solution.py:361
  171.1 0.0 copy-done.3
  171.1 2.8 %convolution_add_fusion = f32[384,1024]{1,0:T(8,128)} fusion(f32[384,1024]{1,0:T(8,128)S(1)} %convolution_add_fusion.1, f32[256,384]{1,0:T(8,128)S(1)} %gain.3, f32[256,1024]{1,0:T(8,128)S(1)} %get-tuple-element.12, bf16[2,256,1024]{2,1,0:T(8,128)(2,1)S(1)} %copy-done.3, f32[256]{0:T(256)S(1)} %sqrt.15, f32[256]{0:T(256)S(1)} %bitcast.34), kind=kOutput, calls=%fused_computation.2 | convolution fusion | flops 1209401344 | bytes 5113856 | tf_op jit(solution)/shard_map/ps,pm->sm/dot_general | solution.py:401
  (18 shorter events, 0.2 us)
Async XLA Ops:
  6.6 43.8 %copy-start = (f32[384,1024]{1,0:T(8,128)S(1)}, f32[384,1024]{1,0:T(8,128)}, u32[]{:S(2)}) copy-start(f32[384,1024]{1,0:T(8,128)} %param.8) | copy-start | bytes 4718596
  52.4 13.8 %copy-start.4 = (f32[2,256]{1,0:T(2,128)S(1)}, f32[2,256]{1,0:T(2,128)}, u32[]{:S(2)}) copy-start(f32[2,256]{1,0:T(2,128)} %param.11) | copy-start | bytes 6148
  65.5 23.9 %copy-start.5 = (f32[2,256]{1,0:T(2,128)S(1)}, f32[2,256]{1,0:T(2,128)}, u32[]{:S(2)}) copy-start(f32[2,256]{1,0:T(2,128)} %param.9) | copy-start | bytes 6148
  65.5 23.9 %copy-start.1 = (f32[384,1024]{1,0:T(8,128)S(1)}, f32[384,1024]{1,0:T(8,128)}, u32[]{:S(2)}) copy-start(f32[384,1024]{1,0:T(8,128)} %param.8) | copy-start | bytes 4718596
  65.5 23.9 %copy-start.2 = (bf16[2,256,1024]{2,1,0:T(8,128)(2,1)S(1)}, bf16[2,256,1024]{2,1,0:T(8,128)(2,1)}, u32[]{:S(2)}) copy-start(bf16[2,256,1024]{2,1,0:T(8,128)(2,1)} %param.10) | copy-start | bytes 3145732
  135.5 35.6 %copy-start.3 = (bf16[2,256,1024]{2,1,0:T(8,128)(2,1)S(1)}, bf16[2,256,1024]{2,1,0:T(8,128)(2,1)}, u32[]{:S(2)}) copy-start(bf16[2,256,1024]{2,1,0:T(8,128)(2,1)} %param.10) | copy-start | bytes 3145732

commit v2 on v1

--- a/solution.py
+++ b/solution.py
@@ -9,7 +9,7 @@
 
 NB = 2
 LAG = 3
-CHUNKS = 16
+CHUNKS = 32
 SUM_CHUNKS = 4
 MESH = pl.DeviceIdType.MESH
 finest = lax.Precision.HIGHEST
@@ -298,7 +298,7 @@
             step_copy(i, c).wait_send()
 
 
-def sum_call(n_ens, part):
+def sum_call(n_ens, part, ident):
     vmem = pl.BlockSpec(memory_space=pltpu.VMEM)
     half = (part.shape[0] // 2, part.shape[1])
     steps = max(1, (n_ens - 1).bit_length() - 1)
@@ -317,7 +317,7 @@
         ]
         + [dma((2, SUM_CHUNKS))] * (2 + steps),
         compiler_params=pltpu.CompilerParams(
-            collective_id=1, has_side_effects=True, vmem_limit_bytes=32 * 2**20
+            collective_id=ident, has_side_effects=True, vmem_limit_bytes=32 * 2**20
         ),
         name="ens_sum",
     )(part)
@@ -329,15 +329,38 @@
 
 def invert(a):
     size = a.shape[0]
-    across = lax.broadcasted_iota(jnp.int32, (1, size), 1)
-    down = lax.broadcasted_iota(jnp.int32, (size, 1), 0)
-    for k in range(size):
-        column = a[:, k : k + 1]
-        pivot = 1.0 / a[k : k + 1, k : k + 1]
-        row = jnp.where(across == k, 1.0, a[k : k + 1, :]) * pivot
-        rest = jnp.where(across == k, 0.0, a) - column * row
-        a = jnp.where(down == k, row, rest)
-    return a
+    across = lax.broadcasted_iota(jnp.int32, (8, size), 1)
+    down = lax.broadcasted_iota(jnp.int32, (8, size), 0)
+    blocks = [a[8 * i : 8 * i + 8, :] for i in range(size // 8)]
+    for k in range(len(blocks)):
+        base = 8 * k
+        panel = blocks[k]
+        columns = [
+            jnp.broadcast_to(panel[:, base + j : base + j + 1], (8, size)) for j in range(8)
+        ]
+        for j in range(8):
+            pivot = 1.0 / columns[j][j : j + 1, :]
+            lead = columns[j]
+            for i in range(8):
+                if i != j:
+                    entry = columns[i][j : j + 1, :] * pivot
+                    columns[i] = jnp.where(down == j, entry, columns[i] - lead * entry)
+            columns[j] = jnp.where(down == j, pivot, -lead * pivot)
+        inside = (across >= base) & (across < base + 8)
+        panel = jnp.where(inside, jnp.where(across - base == down, 1.0, 0.0), panel)
+        terms = [columns[j] * panel[j : j + 1, :] for j in range(8)]
+        while len(terms) > 1:
+            terms = [terms[i] + terms[i + 1] for i in range(0, len(terms), 2)]
+        panel = terms[0]
+        order = list(range(k + 1, len(blocks))) + list(range(k))
+        for i in order:
+            block = blocks[i]
+            terms = [block[:, base + j : base + j + 1] * panel[j : j + 1, :] for j in range(8)]
+            while len(terms) > 1:
+                terms = [terms[m] + terms[m + 1] for m in range(0, len(terms), 2)]
+            blocks[i] = jnp.where(inside, 0.0, block) - terms[0]
+        blocks[k] = panel
+    return jnp.concatenate(blocks, axis=0)
 
 
 def solve_kernel(moments, scale, diagonal, out):
@@ -375,30 +398,45 @@
     members = width * n_ens
     states = rows * n_state
     reach = states // 4
+    size = obs_offset.shape[1]
     here = lax.axis_index("state")
     positions = here * rows + jnp.arange(rows, dtype=jnp.int32)
-    current = ensemble
+    places = owner[:, None] * rows + obs_offset
+
+    masked = jnp.where(
+        jnp.repeat(here == owner, size)[:, None],
+        jnp.take(ensemble, obs_offset.reshape(-1), axis=0),
+        0.0,
+    )
+    noise_sums = jnp.sum(obs_noise[: NB - 1].astype(jnp.float32), axis=2).reshape(-1)
+    sums = jnp.concatenate([jnp.sum(masked, axis=1), jnp.where(here == 0, noise_sums, 0.0)])
+    prior, totals = spread_call(n_state, n_ens, masked, jnp.broadcast_to(sums, (8,) + sums.shape))
+    means = totals[0] / members
+    noise_means = means[NB * size :].reshape(NB - 1, size)
+    means = means[: NB * size].reshape(NB, size)
+    current = jnp.concatenate([prior, ensemble], axis=0)
+    aims = jnp.concatenate([places.reshape(-1), positions])
     for batch in range(NB):
-        places = owner[batch] * rows + obs_offset[batch]
-        aims = jnp.concatenate([places, positions])
-        scale = cycle_taper(places[:, None], aims[None, :], states, reach) / (members - 1)
-        diagonal = jnp.diag(obs_var[batch])
-        local_rows = jnp.take(current, obs_offset[batch], axis=0)
-        masked = jnp.where(here == owner[batch], local_rows, 0.0)
-        sums = jnp.broadcast_to(jnp.sum(masked, axis=1)[None, :], (8, masked.shape[0]))
-        prior, totals = spread_call(n_state, n_ens, masked, sums)
-        anom = prior - (totals[0] / members)[:, None]
+        scale = cycle_taper(places[batch][:, None], aims[None, :], states, reach) / (members - 1)
+        variance = obs_var[batch]
+        prior, current, aims = current[:size], current[size:], aims[size:]
+        anom = prior - means[0][:, None]
         spread = jnp.einsum("pm,qm->pq", anom, anom, precision=finest)
         cross = jnp.einsum("pm,sm->ps", anom, current, precision=finest)
-        moments = sum_call(n_ens, jnp.concatenate([spread, cross], axis=1))
-        gain = solve_call(moments, scale, diagonal)
-        variance = obs_var[batch]
+        moments = sum_call(n_ens, jnp.concatenate([spread, cross], axis=1), 1 + batch)
+        gain = solve_call(moments, scale, jnp.diag(variance))
         misfit = (
             obs_values[batch][:, None]
             + jnp.sqrt(variance)[:, None] * obs_noise[batch].astype(jnp.float32)
             - prior
         )
         current = current + jnp.einsum("ps,pm->sm", gain, misfit, precision=finest)
+        if batch + 1 < NB:
+            misfit_mean = obs_values[batch] + jnp.sqrt(variance) * noise_means[batch] - means[0]
+            later = gain[:, : (NB - 1 - batch) * size]
+            means = means[1:] + jnp.einsum(
+                "ps,p->s", later, misfit_mean, precision=finest
+            ).reshape(-1, size)
     return current
 
 

time: 174 us -> 137 us (0.79)
  Pallas kernels: 153 us -> 113 us
  other arithmetic: 1.47 us -> 4.21 us
  between operations: 2.92 us -> 0.34 us
  matrix products: 10.7 us -> 12.6 us
    pallas_call x2, Pallas kernels: 46.2 us -> 17.6 us  [solve_call(): pl.pallas_call(solve_kernel, out_shape=jax.ShapeDtypeStruct((size, moment...]
    pallas_call x2 -> x1, Pallas kernels: 81.7 us -> 69 us  [spread_call(): pl.pallas_call(functools.partial(spread_kernel, n_state, n_ens), out_shap...]
    slice x3 -> x4, local copies, waits for them, and re-layouts: 2.08 us -> 0.02 us  [the longest x1 0.01 us: local(): places[batch][:, None]]
    pallas_call x2, Pallas kernels: 24.7 us -> 26.7 us  [sum_call(): pl.pallas_call(functools.partial(sum_kernel, n_ens), out_shape=jax.ShapeD...]
    gather x2 -> x1, local copies, waits for them, and re-layouts: 4.05 us -> 5.06 us  [local(): jnp.take(ensemble, obs_offset.reshape(-1), axis=0)]
where the time goes in v2:
time: 137 us; the launch traced here: 136 us
  Pallas kernels  113 us (82%)
  matrix products  12.6 us (9%)
  local copies, waits for them, and re-layouts  5.94 us (4%)
  other arithmetic  4.21 us (3%)
    pallas_call x1, Pallas kernels, spread_call(): pl.pallas_call(functools.partial(spread_kernel, n_state, n_ens), out_shap...  69 us
    pallas_call x2, Pallas kernels, sum_call(): pl.pallas_call(functools.partial(sum_kernel, n_ens), out_shape=jax.ShapeD...  26.7 us
    pallas_call x2, Pallas kernels, solve_call(): pl.pallas_call(solve_kernel, out_shape=jax.ShapeDtypeStruct((size, moment...  17.6 us
    dot_general x2, matrix products, local(): current = current + jnp.einsum('ps,pm->sm', gain, misfit, precision=finest)  5.29 us
    gather x1, local copies, waits for them, and re-layouts, local(): jnp.take(ensemble, obs_offset.reshape(-1), axis=0)  5.06 us
    dot_general x2, matrix products, local(): cross = jnp.einsum('pm,sm->ps', anom, current, precision=finest)  4.8 us

profile of v2, /device:TPU:0, one launch (start us, length us, event | category | flops | bytes accessed | tf_op | source)
XLA Modules:
  0.0 136.4 jit_solution(4736207069037829514)
XLA Ops:
  0.0 0.7 broadcast_compare_fusion
  0.7 0.1 broadcast_in_dim.68
  0.8 0.7 copy.10
  1.5 0.0 copy-start.5
  1.5 5.1 %gather_fusion = f32[512,1024]{1,0:T(8,128)} fusion(f32[384,1024]{1,0:T(8,128)} %param.6, s32[1024]{0:T(1024)S(1)} %pad_clamp_fusion), kind=kCustom, calls=%fused_computation | custom fusion | bytes 4196352 | tf_op jit(solution)/shard_map/jit(_take)/gather | solution.py:408
  6.5 0.0 copy-done.5
  6.5 0.0 copy-start.4
  6.6 2.1 %fusion.46 = (f32[512]{0:T(512)S(1)}, f32[512,1024]{1,0:T(8,128)S(1)}) fusion(f32[512,1024]{1,0:T(8,128)} %gather_fusion, pred[512]{0:T(512)(128)(4,1)S(1)} %compare_and_fusion, pred[512]{0:T(512)(128)(4,1)S(1)} %broadcast_in_dim.69), kind=kLoop, calls=%fused_computation.71 | loop fusion | flops 1572352 | bytes 4197376 | tf_op jit(solution)/shard_map/reduce_sum | solution.py:412
  8.6 0.0 copy-done.4
  8.6 0.0 copy-start.2
  8.7 0.1 convert_reduce_fusion
  8.8 69.0 %spread.1 = (f32[512,1024]{1,0:T(8,128)S(1)}, f32[8,768]{1,0:T(8,128)S(1)}) custom-call(f32[512,1024]{1,0:T(8,128)S(1)} %get-tuple-element.10.own, f32[8,768]{1,0:T(8,128)S(1)} %broadcast_in_dim.75.sums), custom_call_target="tpu_custom_call" | custom-call | tf_op jit(solution)/shard_map/spread/pallas_call | solution.py:207
  77.9 0.0 copy-start
  77.9 1.1 fusion.12
  79.1 0.0 copy-done.2
  79.1 2.9 %fusion = f32[256,640]{1,0:T(8,128)S(1)} fusion(f32[384,1024]{1,0:T(8,128)S(1)} %copy-done.2, f32[512,1024]{1,0:T(8,128)S(1)} %get-tuple-element.7, f32[256]{0:T(256)S(1)} %bitcast.58), kind=kOutput, calls=%fused_computation.4 | convolution fusion | flops 2014183424 | bytes 5374976 | tf_op jit(solution)/shard_map/pm,sm->ps/dot_general | solution.py:425
  81.9 0.0 copy-done
  81.9 0.0 copy-start.8
  82.0 0.0 copy-start.6
  82.0 0.1 pad_maximum_fusion.2.part
  82.0 14.4 %ens_sum.2.moments = f32[256,896]{1,0:T(8,128)S(1)} custom-call(f32[256,896]{1,0:T(8,128)S(1)} %pad_maximum_fusion.2.part), custom_call_target="tpu_custom_call" | custom-call | tf_op jit(solution)/shard_map/ens_sum/pallas_call | solution.py:306
  96.4 0.0 copy-start.7
  96.4 0.0 copy-done.8
  96.4 0.1 fusion.54
  96.5 0.1 broadcast_add_fusion
  96.6 0.0 copy-start.1
  96.6 0.0 copy-start.3
  96.6 0.5 fusion.23.scale
  97.1 0.0 copy-done.6
  97.1 0.1 fusion.44.diagonal
  97.2 8.8 %gain.2 = f32[256,640]{1,0:T(8,128)S(1)} custom-call(f32[256,896]{1,0:T(8,128)S(1)} %ens_sum.2.moments, f32[256,896]{1,0:T(8,128)S(1)} %fusion.23.scale, f32[256,256]{1,0:T(8,128)S(1)} %fusion.44.diagonal), custom_call_target="tpu_custom_call" | custom-call | tf_op jit(solution)/shard_map/gain/pallas_call | solution.py:384
  106.0 0.0 copy-done.7
  106.1 0.2 fusion.41
  106.3 0.0 copy-done.1
  106.3 0.0 copy-done.3
  106.3 2.5 %convolution_add_fusion = f32[640,1024]{1,0:T(8,128)S(1)} fusion(f32[256,640]{1,0:T(8,128)S(1)} %gain.2, f32[384,1024]{1,0:T(8,128)S(1)} %copy-done.3, f32[512,1024]{1,0:T(8,128)S(1)} %copy-done.1, f32[256]{0:T(256)S(1)} %get-tuple-element.21, f32[256]{0:T(256)S(1)} %bitcast.44, bf16[2,256,1024]{2,1,0:T(8,128)(2,1)S(1)} %copy-done.4), kind=kOutput, calls=%fused_computation.3 | convolution fusion | flops 2015625216 | bytes 8521728 | tf_op jit(solution)/shard_map/ps,pm->sm/dot_general | solution.py:433
  108.8 1.1 fusion.14
  110.0 1.9 %fusion.1 = f32[256,384]{1,0:T(8,128)S(1)} fusion(f32[640,1024]{1,0:T(8,128)S(1)} %convolution_add_fusion, f32[256]{0:T(256)S(1)} %add.88), kind=kOutput, calls=%fused_computation.6 | convolution fusion | flops 1208221696 | bytes 3015680 | tf_op jit(solution)/shard_map/pm,sm->ps/dot_general | solution.py:425
  112.0 12.4 %ens_sum.3.moments = f32[256,640]{1,0:T(8,128)S(1)} custom-call(f32[256,640]{1,0:T(8,128)S(1)} %pad_maximum_fusion.3.part), custom_call_target="tpu_custom_call" | custom-call | tf_op jit(solution)/shard_map/ens_sum/pallas_call | solution.py:306
  124.4 0.3 fusion.29.scale
  124.8 0.1 fusion.43.diagonal
  124.9 8.7 %gain.3 = f32[256,384]{1,0:T(8,128)S(1)} custom-call(f32[256,640]{1,0:T(8,128)S(1)} %ens_sum.3.moments, f32[256,640]{1,0:T(8,128)S(1)} %fusion.29.scale, f32[256,256]{1,0:T(8,128)S(1)} %fusion.43.diagonal), custom_call_target="tpu_custom_call" | custom-call | tf_op jit(solution)/shard_map/gain/pallas_call | solution.py:384
  133.6 2.8 %convolution_add_fusion.1 = f32[384,1024]{1,0:T(8,128)} fusion(f32[256,384]{1,0:T(8,128)S(1)} %gain.3, f32[640,1024]{1,0:T(8,128)S(1)} %convolution_add_fusion, bf16[2,256,1024]{2,1,0:T(8,128)(2,1)S(1)} %copy-done.4, f32[256]{0:T(256)S(1)} %sqrt.16, f32[256]{0:T(256)S(1)} %bitcast.53), kind=kOutput, calls=%fused_computation.5 | convolution fusion | flops 1209401344 | bytes 5113856 | tf_op jit(solution)/shard_map/ps,pm->sm/dot_general | solution.py:433
  (22 shorter events, 0.2 us)
Async XLA Ops:
  1.5 5.1 %copy-start.5 = (s32[2,256]{1,0:T(2,128)S(1)}, s32[2,256]{1,0:T(2,128)}, u32[]{:S(2)}) copy-start(s32[2,256]{1,0:T(2,128)} %param.10) | copy-start | bytes 6148
  6.5 2.1 %copy-start.4 = (bf16[2,256,1024]{2,1,0:T(8,128)(2,1)S(1)}, bf16[2,256,1024]{2,1,0:T(8,128)(2,1)}, u32[]{:S(2)}) copy-start(bf16[2,256,1024]{2,1,0:T(8,128)(2,1)} %param.8) | copy-start | bytes 3145732
  8.6 70.4 %copy-start.2 = (f32[384,1024]{1,0:T(8,128)S(1)}, f32[384,1024]{1,0:T(8,128)}, u32[]{:S(2)}) copy-start(f32[384,1024]{1,0:T(8,128)} %param.6) | copy-start | bytes 4718596
  77.9 4.1 %copy-start = (f32[512,1024]{1,0:T(8,128)}, f32[512,1024]{1,0:T(8,128)S(1)}, u32[]{:S(2)}) copy-start(f32[512,1024]{1,0:T(8,128)S(1)} %get-tuple-element.7) | copy-start | bytes 6291460
  81.9 14.5 %copy-start.8 = (s32[2]{0:T(128)S(1)}, s32[2]{0:T(128)}, u32[]{:S(2)}) copy-start(s32[2]{0:T(128)} %param.11) | copy-start | bytes 28
  82.0 15.1 %copy-start.6 = (f32[2,256]{1,0:T(2,128)S(1)}, f32[2,256]{1,0:T(2,128)}, u32[]{:S(2)}) copy-start(f32[2,256]{1,0:T(2,128)} %param.9) | copy-start | bytes 6148
  96.4 9.6 %copy-start.7 = (f32[2,256]{1,0:T(2,128)S(1)}, f32[2,256]{1,0:T(2,128)}, u32[]{:S(2)}) copy-start(f32[2,256]{1,0:T(2,128)} %param.7) | copy-start | bytes 6148
  96.6 9.7 %copy-start.1 = (f32[512,1024]{1,0:T(8,128)S(1)}, f32[512,1024]{1,0:T(8,128)}, u32[]{:S(2)}) copy-start(f32[512,1024]{1,0:T(8,128)} %copy-done) | copy-start | bytes 6291460
  96.6 9.7 %copy-start.3 = (f32[384,1024]{1,0:T(8,128)S(1)}, f32[384,1024]{1,0:T(8,128)}, u32[]{:S(2)}) copy-start(f32[384,1024]{1,0:T(8,128)} %param.6) | copy-start | bytes 4718596

commit v3 on v2

--- a/solution.py
+++ b/solution.py
@@ -8,9 +8,9 @@
 from jax.sharding import PartitionSpec as P
 
 NB = 2
-LAG = 3
-CHUNKS = 32
-SUM_CHUNKS = 4
+LAG = 4
+CHUNKS = 64
+SUM_CHUNKS = 8
 MESH = pl.DeviceIdType.MESH
 finest = lax.Precision.HIGHEST
 
@@ -430,7 +430,9 @@
             + jnp.sqrt(variance)[:, None] * obs_noise[batch].astype(jnp.float32)
             - prior
         )
-        current = current + jnp.einsum("ps,pm->sm", gain, misfit, precision=finest)
+        current = current + jnp.einsum(
+            "ps,pm->sm", gain, misfit, precision=lax.Precision.HIGH
+        )
         if batch + 1 < NB:
             misfit_mean = obs_values[batch] + jnp.sqrt(variance) * noise_means[batch] - means[0]
             later = gain[:, : (NB - 1 - batch) * size]

time: 137 us -> 136 us (level)
  Pallas kernels: 113 us -> 115 us
  matrix products: 12.6 us -> 10.9 us
    dot_general x2, matrix products: 5.29 us -> 3.56 us  [local(): jnp.einsum('ps,pm->sm', gain, misfit, precision=lax.Precision.HIGH)]
where the time goes in v3:
time: 136 us
  Pallas kernels  115 us (85%)
  matrix products  10.9 us (8%)
  local copies, waits for them, and re-layouts  5.94 us (4%)
  other arithmetic  4.21 us (3%)
    pallas_call x1, Pallas kernels, spread_call(): pl.pallas_call(functools.partial(spread_kernel, n_state, n_ens), out_shap...  70 us
    pallas_call x2, Pallas kernels, sum_call(): pl.pallas_call(functools.partial(sum_kernel, n_ens), out_shape=jax.ShapeD...  27 us
    pallas_call x2, Pallas kernels, solve_call(): pl.pallas_call(solve_kernel, out_shape=jax.ShapeDtypeStruct((size, moment...  17.6 us
    gather x1, local copies, waits for them, and re-layouts, local(): jnp.take(ensemble, obs_offset.reshape(-1), axis=0)  5.06 us
    dot_general x2, matrix products, local(): cross = jnp.einsum('pm,sm->ps', anom, current, precision=finest)  4.8 us
    dot_general x2, matrix products, local(): jnp.einsum('ps,pm->sm', gain, misfit, precision=lax.Precision.HIGH)  3.56 us

profile of v3, /device:TPU:0, one launch (start us, length us, event | category | flops | bytes accessed | tf_op | source)
XLA Modules:
  0.0 135.9 jit_solution(9975102621769095696)
XLA Ops:
  0.0 0.7 broadcast_compare_fusion
  0.7 0.1 broadcast_in_dim.68
  0.8 0.7 copy.10
  1.5 0.0 copy-start.5
  1.5 5.1 %gather_fusion = f32[512,1024]{1,0:T(8,128)} fusion(f32[384,1024]{1,0:T(8,128)} %param.6, s32[1024]{0:T(1024)S(1)} %pad_clamp_fusion), kind=kCustom, calls=%fused_computation | custom fusion | bytes 4196352 | tf_op jit(solution)/shard_map/jit(_take)/gather | solution.py:408
  6.5 0.0 copy-done.5
  6.5 0.0 copy-start.4
  6.6 2.1 %fusion.46 = (f32[512]{0:T(512)S(1)}, f32[512,1024]{1,0:T(8,128)S(1)}) fusion(f32[512,1024]{1,0:T(8,128)} %gather_fusion, pred[512]{0:T(512)(128)(4,1)S(1)} %compare_and_fusion, pred[512]{0:T(512)(128)(4,1)S(1)} %broadcast_in_dim.69), kind=kLoop, calls=%fused_computation.71 | loop fusion | flops 1572352 | bytes 4197376 | tf_op jit(solution)/shard_map/reduce_sum | solution.py:412
  8.6 0.0 copy-done.4
  8.6 0.0 copy-start.2
  8.7 0.1 convert_reduce_fusion
  8.8 70.0 %spread.1 = (f32[512,1024]{1,0:T(8,128)S(1)}, f32[8,768]{1,0:T(8,128)S(1)}) custom-call(f32[512,1024]{1,0:T(8,128)S(1)} %get-tuple-element.10.own, f32[8,768]{1,0:T(8,128)S(1)} %broadcast_in_dim.75.sums), custom_call_target="tpu_custom_call" | custom-call | tf_op jit(solution)/shard_map/spread/pallas_call | solution.py:207
  78.8 0.0 copy-start
  78.9 1.1 fusion.12
  80.0 0.0 copy-done.2
  80.0 2.8 %fusion = f32[256,640]{1,0:T(8,128)S(1)} fusion(f32[384,1024]{1,0:T(8,128)S(1)} %copy-done.2, f32[512,1024]{1,0:T(8,128)S(1)} %get-tuple-element.7, f32[256]{0:T(256)S(1)} %bitcast.58), kind=kOutput, calls=%fused_computation.4 | convolution fusion | flops 2014183424 | bytes 5374976 | tf_op jit(solution)/shard_map/pm,sm->ps/dot_general | solution.py:425
  82.9 0.0 copy-done
  82.9 0.0 copy-start.8
  82.9 0.0 copy-start.6
  82.9 0.1 pad_maximum_fusion.2.part
  83.0 14.5 %ens_sum.2.moments = f32[256,896]{1,0:T(8,128)S(1)} custom-call(f32[256,896]{1,0:T(8,128)S(1)} %pad_maximum_fusion.2.part), custom_call_target="tpu_custom_call" | custom-call | tf_op jit(solution)/shard_map/ens_sum/pallas_call | solution.py:306
  97.5 0.0 copy-start.7
  97.5 0.0 copy-done.8
  97.5 0.1 fusion.54
  97.6 0.1 broadcast_add_fusion
  97.7 0.0 copy-start.1
  97.7 0.0 copy-start.3
  97.7 0.5 fusion.23.scale
  98.2 0.0 copy-done.6
  98.2 0.1 fusion.44.diagonal
  98.3 8.8 %gain.2 = f32[256,640]{1,0:T(8,128)S(1)} custom-call(f32[256,896]{1,0:T(8,128)S(1)} %ens_sum.2.moments, f32[256,896]{1,0:T(8,128)S(1)} %fusion.23.scale, f32[256,256]{1,0:T(8,128)S(1)} %fusion.44.diagonal), custom_call_target="tpu_custom_call" | custom-call | tf_op jit(solution)/shard_map/gain/pallas_call | solution.py:384
  107.1 0.0 copy-done.7
  107.2 0.2 fusion.41
  107.4 0.0 copy-done.1
  107.4 0.0 copy-done.3
  107.4 1.4 %convolution_add_fusion = f32[640,1024]{1,0:T(8,128)S(1)} fusion(f32[256,640]{1,0:T(8,128)S(1)} %gain.2, f32[384,1024]{1,0:T(8,128)S(1)} %copy-done.3, f32[512,1024]{1,0:T(8,128)S(1)} %copy-done.1, f32[256]{0:T(256)S(1)} %get-tuple-element.21, f32[256]{0:T(256)S(1)} %bitcast.44, bf16[2,256,1024]{2,1,0:T(8,128)(2,1)S(1)} %copy-done.4), kind=kOutput, calls=%fused_computation.3 | convolution fusion | flops 1008992256 | bytes 8521728 | tf_op jit(solution)/shard_map/ps,pm->sm/dot_general | solution.py:433
  108.8 1.1 fusion.14
  110.0 1.9 %fusion.1 = f32[256,384]{1,0:T(8,128)S(1)} fusion(f32[640,1024]{1,0:T(8,128)S(1)} %convolution_add_fusion, f32[256]{0:T(256)S(1)} %add.88), kind=kOutput, calls=%fused_computation.6 | convolution fusion | flops 1208221696 | bytes 3015680 | tf_op jit(solution)/shard_map/pm,sm->ps/dot_general | solution.py:425
  112.0 12.5 %ens_sum.3.moments = f32[256,640]{1,0:T(8,128)S(1)} custom-call(f32[256,640]{1,0:T(8,128)S(1)} %pad_maximum_fusion.3.part), custom_call_target="tpu_custom_call" | custom-call | tf_op jit(solution)/shard_map/ens_sum/pallas_call | solution.py:306
  124.5 0.3 fusion.29.scale
  124.9 0.1 fusion.43.diagonal
  125.0 8.7 %gain.3 = f32[256,384]{1,0:T(8,128)S(1)} custom-call(f32[256,640]{1,0:T(8,128)S(1)} %ens_sum.3.moments, f32[256,640]{1,0:T(8,128)S(1)} %fusion.29.scale, f32[256,256]{1,0:T(8,128)S(1)} %fusion.43.diagonal), custom_call_target="tpu_custom_call" | custom-call | tf_op jit(solution)/shard_map/gain/pallas_call | solution.py:384
  133.7 2.2 %convolution_add_fusion.1 = f32[384,1024]{1,0:T(8,128)} fusion(f32[256,384]{1,0:T(8,128)S(1)} %gain.3, f32[640,1024]{1,0:T(8,128)S(1)} %convolution_add_fusion, bf16[2,256,1024]{2,1,0:T(8,128)(2,1)S(1)} %copy-done.4, f32[256]{0:T(256)S(1)} %sqrt.16, f32[256]{0:T(256)S(1)} %bitcast.53), kind=kOutput, calls=%fused_computation.5 | convolution fusion | flops 605421568 | bytes 5113856 | tf_op jit(solution)/shard_map/ps,pm->sm/dot_general | solution.py:433
  (22 shorter events, 0.2 us)
Async XLA Ops:
  1.5 5.1 %copy-start.5 = (s32[2,256]{1,0:T(2,128)S(1)}, s32[2,256]{1,0:T(2,128)}, u32[]{:S(2)}) copy-start(s32[2,256]{1,0:T(2,128)} %param.10) | copy-start | bytes 6148
  6.5 2.1 %copy-start.4 = (bf16[2,256,1024]{2,1,0:T(8,128)(2,1)S(1)}, bf16[2,256,1024]{2,1,0:T(8,128)(2,1)}, u32[]{:S(2)}) copy-start(bf16[2,256,1024]{2,1,0:T(8,128)(2,1)} %param.8) | copy-start | bytes 3145732
  8.6 71.4 %copy-start.2 = (f32[384,1024]{1,0:T(8,128)S(1)}, f32[384,1024]{1,0:T(8,128)}, u32[]{:S(2)}) copy-start(f32[384,1024]{1,0:T(8,128)} %param.6) | copy-start | bytes 4718596
  78.8 4.1 %copy-start = (f32[512,1024]{1,0:T(8,128)}, f32[512,1024]{1,0:T(8,128)S(1)}, u32[]{:S(2)}) copy-start(f32[512,1024]{1,0:T(8,128)S(1)} %get-tuple-element.7) | copy-start | bytes 6291460
  82.9 14.6 %copy-start.8 = (s32[2]{0:T(128)S(1)}, s32[2]{0:T(128)}, u32[]{:S(2)}) copy-start(s32[2]{0:T(128)} %param.11) | copy-start | bytes 28
  82.9 15.3 %copy-start.6 = (f32[2,256]{1,0:T(2,128)S(1)}, f32[2,256]{1,0:T(2,128)}, u32[]{:S(2)}) copy-start(f32[2,256]{1,0:T(2,128)} %param.9) | copy-start | bytes 6148
  97.5 9.6 %copy-start.7 = (f32[2,256]{1,0:T(2,128)S(1)}, f32[2,256]{1,0:T(2,128)}, u32[]{:S(2)}) copy-start(f32[2,256]{1,0:T(2,128)} %param.7) | copy-start | bytes 6148
  97.7 9.7 %copy-start.1 = (f32[512,1024]{1,0:T(8,128)S(1)}, f32[512,1024]{1,0:T(8,128)}, u32[]{:S(2)}) copy-start(f32[512,1024]{1,0:T(8,128)} %copy-done) | copy-start | bytes 6291460
  97.7 9.7 %copy-start.3 = (f32[384,1024]{1,0:T(8,128)S(1)}, f32[384,1024]{1,0:T(8,128)}, u32[]{:S(2)}) copy-start(f32[384,1024]{1,0:T(8,128)} %param.6) | copy-start | bytes 4718596
